TPU v7x, 128 devices: a whole 4x4x4 slice. The times are simulated.
128 devices in a mesh: req: 64 (over y, x, z), head: 2 (over core).
Axes of the slice: x: 4, y: 4, z: 4, core: 2. Of those that a mesh axis runs over, the one named last changes fastest.
Arguments:
- hidden_in: bfloat16 [4096, 2048], P('req'), may hold values from -14 to 14
- attn_gain: float32 [2048], replicated, may hold values from 0.1 to 1.9
- w_query: bfloat16 [2048, 2048], P(None, 'head'), may hold values from -0.125 to 0.125
- w_key: bfloat16 [2048, 1024], P(None, 'head'), may hold values from -0.125 to 0.125
- w_value: bfloat16 [2048, 1024], P(None, 'head'), may hold values from -0.125 to 0.125
- query_gain: float32 [128], replicated, may hold values from 0.5 to 2
- key_gain: float32 [128], replicated, may hold values from 0.5 to 2
- w_out: bfloat16 [2048, 2048], P('head'), may hold values from -0.125 to 0.125
- cache_keys: bfloat16 [64, 2048, 1024], P('req', None, 'head'), may hold values from -3.5 to 3.5
- cache_values: bfloat16 [64, 2048, 1024], P('req', None, 'head'), may hold values from -6 to 6
- cache_lengths: int32 [64], replicated, may hold values from 1 to 2048, 65536 in all
- slot_request: int32 [64], replicated, may hold values from 0 to 63, each once
- mlp_gain: float32 [2048], P('head'), may hold values from 0.1 to 1.9
- w_gate: bfloat16 [2048, 6144], P('head', 'req'), may hold values from -0.125 to 0.125
- w_up: bfloat16 [2048, 6144], P('head', 'req'), may hold values from -0.125 to 0.125
- w_down: bfloat16 [6144, 2048], P('req', 'head'), may hold values from -0.078125 to 0.078125
- final_gain: float32 [2048], replicated, may hold values from 0.1 to 1.9
- w_vocab: bfloat16 [2048, 151936], P(None, ('req', 'head')), may hold values from -8 to 8
Outputs:
- hidden_out: bfloat16 [4096, 2048], P('req', 'head')
- log_probs: float32 [64, 151936], P(None, ('req', 'head'))
Inputs may be any that keep to these rules, and one draw needn't show every extreme that they name: `cache_lengths`: the largest length is exactly 2048. `slot_request`: each request appears once.
All inputs are finite; a program needn't handle non-finite values.
Results may differ from a plain program's by a relative error of at most 0.008.
Values may be sent and summed in bfloat16 or wider, within the bound.
A program may use at most 128 MiB of HBM per device.

v0:
```python
import jax
import jax.numpy as jnp
from jax import lax
from jax.sharding import PartitionSpec as P

D = 2048
HEAD_DIM = 128
EPS = 1e-06
ROPE_BASE = 1000000.0
NEG = -1e30


def norm_rows(field, gain_vec):
    return field * lax.rsqrt(jnp.mean(field * field, axis=-1, keepdims=True) + EPS) * gain_vec


def rotate(field, positions):
    half_dim = field.shape[-1] // 2
    frequency = ROPE_BASE ** (-2.0 * jnp.arange(half_dim, dtype=jnp.float32) / field.shape[-1])
    angles = positions[..., None, None] * frequency
    cosine = jnp.cos(angles)
    sines = jnp.sin(angles)
    lower_half = field[..., :half_dim]
    upper_half = field[..., half_dim:]
    return jnp.concatenate(
        [lower_half * cosine - upper_half * sines, upper_half * cosine + lower_half * sines],
        axis=-1,
    )


def inverse_order(slot_request):
    indices = jnp.arange(slot_request.shape[0], dtype=jnp.int32)
    return jnp.sum(
        jnp.where(slot_request[None, :] == indices[:, None], indices[None, :], 0), axis=1
    )


def attend_slot(queries, keys_new, values_new, keys_cache, values_cache, cache_len):
    row_count, value_heads, head_size = keys_new.shape
    group_size = queries.shape[1] // value_heads
    grouped = queries.reshape(row_count, value_heads, group_size, head_size)
    score_scale = head_size ** (-0.5)
    recent = (
        jnp.einsum("skgd,tkd->kgst", grouped, keys_new, preferred_element_type=jnp.float32)
        * score_scale
    )
    causal = jnp.arange(row_count)[:, None] >= jnp.arange(row_count)[None, :]
    recent = jnp.where(causal, recent, NEG)
    cache_span = keys_cache.shape[0]
    stored = (
        jnp.einsum("skgd,lkd->kgsl", grouped, keys_cache, preferred_element_type=jnp.float32)
        * score_scale
    )
    stored = jnp.where(jnp.arange(cache_span, dtype=jnp.int32) < cache_len, stored, NEG)
    old_weights = jnp.exp(stored)
    new_weights = jnp.exp(recent)
    row_total = jnp.sum(old_weights, axis=-1) + jnp.sum(new_weights, axis=-1)
    old_weights = (old_weights / row_total[..., None]).astype(jnp.bfloat16)
    new_weights = (new_weights / row_total[..., None]).astype(jnp.bfloat16)
    blended = jnp.einsum(
        "kgsl,lkd->skgd", old_weights, values_cache, preferred_element_type=jnp.float32
    )
    blended = blended + jnp.einsum(
        "kgst,tkd->skgd", new_weights, values_new, preferred_element_type=jnp.float32
    )
    return blended.reshape(row_count, value_heads * group_size * head_size).astype(jnp.bfloat16)


def on_device(
    hidden_in,
    attn_gain,
    w_query,
    w_key,
    w_value,
    query_gain,
    key_gain,
    w_out,
    cache_keys,
    cache_values,
    cache_lengths,
    slot_request,
    mlp_gain,
    w_gate,
    w_up,
    w_down,
    final_gain,
    w_vocab,
):
    row_count = hidden_in.shape[0]
    half_width = mlp_gain.shape[0]
    slot_index = lax.axis_index("req")
    request_id = lax.dynamic_index_in_dim(slot_request, slot_index, 0, keepdims=False)
    cache_len = lax.dynamic_index_in_dim(cache_lengths, request_id, 0, keepdims=False)
    tokens = hidden_in.astype(jnp.float32)
    normed = norm_rows(tokens, attn_gain).astype(jnp.bfloat16)
    query_heads = w_query.shape[1] // HEAD_DIM
    value_heads = w_key.shape[1] // HEAD_DIM
    positions = (cache_len + jnp.arange(row_count, dtype=jnp.int32)).astype(jnp.float32)
    queries = jnp.dot(normed, w_query, preferred_element_type=jnp.float32).reshape(
        row_count, query_heads, HEAD_DIM
    )
    queries = rotate(norm_rows(queries, query_gain), positions).astype(jnp.bfloat16)
    keys_new = jnp.dot(normed, w_key, preferred_element_type=jnp.float32).reshape(
        row_count, value_heads, HEAD_DIM
    )
    keys_new = rotate(norm_rows(keys_new, key_gain), positions).astype(jnp.bfloat16)
    values_new = (
        jnp.dot(normed, w_value, preferred_element_type=jnp.float32)
        .astype(jnp.bfloat16)
        .reshape(row_count, value_heads, HEAD_DIM)
    )
    keys_cache = cache_keys.reshape(cache_keys.shape[1], value_heads, HEAD_DIM)
    values_cache = cache_values.reshape(cache_values.shape[1], value_heads, HEAD_DIM)
    attended = attend_slot(queries, keys_new, values_new, keys_cache, values_cache, cache_len)
    projected = jnp.dot(attended, w_out, preferred_element_type=jnp.float32)
    own_sum = lax.psum_scatter(
        projected.astype(jnp.bfloat16), "head", scatter_dimension=1, tiled=True
    ).astype(jnp.float32)
    head_part = lax.axis_index("head")
    residual = lax.dynamic_slice_in_dim(tokens, head_part * half_width, half_width, 1) + own_sum
    squares = lax.psum(jnp.sum(residual * residual, axis=1), "head")
    mixed_rows = (residual * lax.rsqrt(squares[:, None] / D + EPS) * mlp_gain).astype(jnp.bfloat16)
    paired = jnp.concatenate([w_gate, w_up], axis=1)
    partial_rows = jnp.dot(
        lax.all_gather(mixed_rows, "req", axis=0, tiled=True),
        paired,
        preferred_element_type=jnp.float32,
    )
    summed_rows = lax.psum(partial_rows.astype(jnp.bfloat16), "head").astype(jnp.float32)
    unit_count = w_gate.shape[1]
    active = (jax.nn.silu(summed_rows[:, :unit_count]) * summed_rows[:, unit_count:]).astype(
        jnp.bfloat16
    )
    down_part = lax.psum_scatter(
        jnp.dot(active, w_down, preferred_element_type=jnp.float32),
        "req",
        scatter_dimension=0,
        tiled=True,
    )
    output = residual + down_part
    hidden_out = output.astype(jnp.bfloat16)
    last_row = output[row_count - 1 :, :]
    collected = lax.all_gather(last_row, ("req", "head"), axis=1, tiled=True).reshape(-1, D)
    final_rows = norm_rows(collected, final_gain).astype(jnp.bfloat16)
    logits = jnp.dot(final_rows, w_vocab, preferred_element_type=jnp.float32)
    row_max = lax.pmax(jnp.max(logits, axis=1), ("req", "head"))
    row_total = lax.psum(jnp.sum(jnp.exp(logits - row_max[:, None]), axis=1), ("req", "head"))
    log_probs = logits - row_max[:, None] - jnp.log(row_total)[:, None]
    log_probs = jnp.take(log_probs, inverse_order(slot_request), axis=0)
    return (hidden_out, log_probs)


def solution(mesh):
    in_specs = (
        P("req", None),
        P(),
        P(None, "head"),
        P(None, "head"),
        P(None, "head"),
        P(),
        P(),
        P("head", None),
        P("req", None, "head"),
        P("req", None, "head"),
        P(),
        P(),
        P("head"),
        P("head", "req"),
        P("head", "req"),
        P("req", "head"),
        P(),
        P(None, ("req", "head")),
    )
    out_specs = (P("req", "head"), P(None, ("req", "head")))
    return jax.shard_map(
        on_device, mesh=mesh, in_specs=in_specs, out_specs=out_specs, check_vma=False
    )
```

profile of v0, /device:TPU:1, one launch (start us, length us, event | category | flops | bytes accessed | tf_op | source)
XLA Modules:
  0.0 747.4 jit_solution(8484590395757010456)
XLA Ops:
  7.2 0.0 copy-start
  7.2 0.0 reduce-scatter.3.cloned.1.call-start
  7.2 1.4 dynamic_slice.11
  10.6 1.2 dynamic_slice.12
  11.8 0.6 add_convert_fusion.2
  12.5 0.7 iota_compare_fusion.2
  13.2 1.1 multiply_reduce_fusion.1
  14.3 3.2 convolution_bitcast_fusion
  17.5 0.1 multiply_reduce_fusion.3
  17.7 0.0 copy-start.2
  17.7 0.1 copy.63
  17.8 0.1 copy.64
  17.9 0.2 multiply_cosine_fusion
  18.1 0.1 multiply_multiply_fusion
  18.2 0.2 subtract_convert_fusion
  18.5 4.0 reshape.165
  22.5 0.5 fusion.40
  23.0 0.1 multiply_reduce_fusion.4
  23.2 0.1 copy.68
  23.3 0.1 fusion.27
  23.4 0.1 subtract_convert_fusion.1
  23.5 4.1 reshape.167
  27.6 0.5 convolution_convert_fusion.2
  28.1 3.2 bitcast_reduce_fusion
  31.4 0.3 fusion.43
  31.8 1.4 fusion.12
  33.2 0.2 fusion.17
  33.4 0.1 copy.73
  33.6 0.0 copy-start.9
  33.6 0.1 convert_element_type.62
  33.7 0.0 copy-start.13
  33.7 3.8 convolution_convert_fusion.1
  37.5 0.0 reduce-scatter.3.cloned.1.call-update
  37.5 0.0 all-gather.2.cloned.1.call-start
  37.6 14.1 %reduce-scatter.3.cloned.1.call-done = bf16[64,1024]{1,0:T(8,128)(2,1)} async-done(((bf16[64,2048]{1,0:T(8,128)(2,1)}), bf16[64,1024]{1,0:T(8,128)(2,1)}) %reduce-scatter.3.cloned.1.call-update) | async-done | bytes 131088 | tf_op jit(solution)/shard_map/reduce_scatter | solution.py:116
  51.6 1.0 multiply_reduce_fusion.2
  52.7 2.5 psum.21
  55.2 1.7 multiply_convert_fusion.3
  56.8 0.0 all-gather.2.cloned.1.call-update
  56.9 0.0 all-reduce.2.cloned.1.call-start
  56.9 79.7 %all-gather.2.cloned.1.call-done = bf16[4096,1024]{1,0:T(8,128)(2,1)} async-done(((bf16[64,1024]{1,0:T(8,128)(2,1)}), bf16[4096,1024]{1,0:T(8,128)(2,1)}) %all-gather.2.cloned.1.call-update) | async-done | bytes 8388624 | tf_op jit(solution)/shard_map/all_gather | solution.py:125
  136.6 7.5 %convolution_convert_fusion = bf16[4096,192]{0,1:T(8,128)(2,1)} fusion(bf16[4096,1024]{1,0:T(8,128)(2,1)} %all-gather.2.cloned.1.call-done, bf16[1024,96]{0,1:T(8,128)(2,1)S(1)} %copy-done.12, bf16[1024,96]{0,1:T(8,128)(2,1)S(1)} %copy-done.13), kind=kOutput, calls=%fused_computation.1 | convolution fusion | flops 1612185600 | bytes 10354688 | tf_op jit(solution)/shard_map/dot_general | solution.py:124
  144.2 0.0 all-reduce.2.cloned.1.call-update
  144.2 0.0 reduce-scatter.5.cloned.1.call-start
  144.2 26.1 %all-reduce.2.cloned.1.call-done = bf16[4096,192]{0,1:T(8,128)(2,1)} async-done(((bf16[4096,192]{0,1:T(8,128)(2,1)}), bf16[4096,192]{0,1:T(8,128)(2,1)}) %all-reduce.2.cloned.1.call-update) | async-done | bytes 1572880 | tf_op jit(solution)/shard_map/psum | solution.py:129
  170.3 1.8 convert_element_type.67
  172.1 8.1 %fusion.18 = f32[4096,1024]{1,0:T(8,128)} fusion(bf16[96,1024]{1,0:T(8,128)(2,1)S(1)} %copy-done.6, f32[4096,192]{0,1:T(8,128)S(1)} %convert_element_type.67), kind=kOutput, calls=%fused_computation.24 | convolution fusion | flops 807665664 | bytes 20119552 | tf_op jit(solution)/shard_map/dot_general | solution.py:135
  180.2 0.0 reduce-scatter.5.cloned.1.call-update
  180.2 0.6 copy-done.14
  180.9 0.1 select_reduce_fusion
  181.0 339.7 %reduce-scatter.5.cloned.1.call-done = f32[64,1024]{1,0:T(8,128)} async-done(((f32[4096,1024]{1,0:T(8,128)}), f32[64,1024]{1,0:T(8,128)}) %reduce-scatter.5.cloned.1.call-update) | async-done | bytes 262160 | tf_op jit(solution)/shard_map/reduce_scatter | solution.py:134
  520.7 1.6 fusion.41
  522.4 81.9 %all_gather.7 = f32[1,131072]{1,0:T(1,128)S(1)} all-gather(f32[1,1024]{1,0:T(1,128)S(1)} %slice.36), channel_id=1, replica_groups=mesh['req'=64,'head'=2] {'req','head'}, dimensions={1}, use_global_device_ids=true | all-gather | bytes 528384 | tf_op jit(solution)/shard_map/all_gather | solution.py:143
  604.2 0.5 broadcast.162
  604.8 1.9 reduce.3
  606.6 0.1 reshape.169
  606.7 0.1 multiply_reduce_fusion
  606.9 4.2 fusion.44
  611.1 63.7 %pmax.7 = f32[64]{0:T(128)S(1)} all-reduce(f32[64]{0:T(128)S(1)} %get-tuple-element.14), channel_id=1, replica_groups=mesh['req'=64,'head'=2] {'req','head'}, use_global_device_ids=true, to_apply=%region_13.14 | all-reduce | flops 64 | bytes 512 | tf_op jit(solution)/shard_map/pmax | solution.py:146
  674.8 0.2 exponential_reduce_fusion
  675.0 64.2 %psum.23 = f32[64]{0:T(128)S(1)} all-reduce(f32[64]{0:T(128)S(1)} %exponential_reduce_fusion), channel_id=1, replica_groups=mesh['req'=64,'head'=2] {'req','head'}, use_global_device_ids=true, to_apply=%region_15.16 | all-reduce | flops 64 | bytes 512 | tf_op jit(solution)/shard_map/psum | solution.py:147
  739.2 0.1 subtract_subtract_fusion
  739.3 0.7 gather_fusion
  740.0 0.8 broadcast_select_fusion
  (44 shorter events, 0.4 us)
Async XLA Ops:
  7.2 15.3 %copy-start = (bf16[2048,512]{1,0:T(8,128)(2,1)S(1)}, bf16[2048,512]{1,0:T(8,128)(2,1)}, u32[]{:S(2)}) copy-start(bf16[2048,512]{1,0:T(8,128)(2,1)} %param.21) | copy-start | bytes 6291460
  7.2 10.9 %copy-start.10 = (f32[128]{0:T(128)S(1)}, f32[128]{0:T(128)}, u32[]{:S(2)}) copy-start(f32[128]{0:T(128)} %param.23) | copy-start | bytes 1540
  7.2 44.5 %reduce-scatter.3.cloned.1.call-start = ((), (), s32[]{:S(2)}) async-start(), calls=%async_computation.2 | async-start | bytes 393216 | tf_op jit(solution)/shard_map/reduce_scatter | solution.py:116
  17.7 4.8 copy-start.2
  17.7 4.8 copy-start.7
  18.4 4.8 copy-start.11
  23.0 4.6 copy-start.3
  28.1 3.6 copy-start.4
  33.6 21.6 %copy-start.9 = (f32[1024]{0:T(1024)S(1)}, f32[1024]{0:T(1024)}, u32[]{:S(2)}) copy-start(f32[1024]{0:T(1024)} %param.30) | copy-start | bytes 12292
  33.6 103.0 %copy-start.12 = (bf16[1024,96]{0,1:T(8,128)(2,1)S(1)}, bf16[1024,96]{0,1:T(8,128)(2,1)}, u32[]{:S(2)}) copy-start(bf16[1024,96]{0,1:T(8,128)(2,1)} %param.32) | copy-start | bytes 589828
  33.7 103.0 %copy-start.13 = (bf16[1024,96]{0,1:T(8,128)(2,1)S(1)}, bf16[1024,96]{0,1:T(8,128)(2,1)}, u32[]{:S(2)}) copy-start(bf16[1024,96]{0,1:T(8,128)(2,1)} %param.31) | copy-start | bytes 589828
  37.5 99.2 %all-gather.2.cloned.1.call-start = ((), (), s32[]{:S(2)}) async-start(), calls=%async_computation.3 | async-start | bytes 8519680 | tf_op jit(solution)/shard_map/all_gather | solution.py:125
  56.9 113.5 %all-reduce.2.cloned.1.call-start = ((), (), s32[]{:S(2)}) async-start(), calls=%async_computation.4 | async-start | bytes 3145728 | tf_op jit(solution)/shard_map/psum | solution.py:129
  144.2 27.9 %copy-start.6 = (bf16[96,1024]{1,0:T(8,128)(2,1)S(1)}, bf16[96,1024]{1,0:T(8,128)(2,1)}, u32[]{:S(2)}) copy-start(bf16[96,1024]{1,0:T(8,128)(2,1)} %param.33) | copy-start | bytes 589828
  144.2 376.5 %reduce-scatter.5.cloned.1.call-start = ((), (), s32[]{:S(2)}) async-start(), calls=%async_computation.5 | async-start | bytes 17039360 | tf_op jit(solution)/shard_map/reduce_scatter | solution.py:134
  180.2 0.7 copy-start.14
  180.2 340.5 %copy-start.5 = (bf16[64,1024]{1,0:T(8,128)(2,1)S(1)}, bf16[64,1024]{1,0:T(8,128)(2,1)}, u32[]{:S(2)}) copy-start(bf16[64,1024]{1,0:T(8,128)(2,1)} %reduce-scatter.3.cloned.1.call-done) | copy-start | bytes 393220
  180.9 426.0 %copy-start.8 = (f32[2048]{0:T(1024)S(1)}, f32[2048]{0:T(1024)}, u32[]{:S(2)}) copy-start(f32[2048]{0:T(1024)} %param.34) | copy-start | bytes 24580
  606.9 133.9 %copy-start.1 = (bf16[2048,512]{1,0:T(8,128)(2,1)S(1)}, bf16[2048,512]{1,0:T(8,128)(2,1)}, u32[]{:S(2)}) copy-start(bf16[2048,512]{1,0:T(8,128)(2,1)} %param.21) | copy-start | bytes 6291460
Sparse Core Ops, SparseCore 0:
  37.6 13.9 reduce-scatter.2
  57.0 79.6 all-gather.1
  144.3 25.9 all-reduce.1
  180.4 340.3 reduce-scatter.4
where the time goes:
time: 748 us; the launch traced here: 747 us
  waiting for transfers between devices  460 us (61%)
  blocking collectives  212 us (28%)
  matrix products  33.1 us (4%)
  between operations  16.1 us (2%)
  local copies, waits for them, and re-layouts  13.3 us (2%)
  other arithmetic  12.9 us (2%)
    reduce_scatter x1, waiting for transfers between devices, on_device(): lax.psum_scatter(jnp.dot(active, w_down, preferred_element_type=jnp.float...  340 us
    all_gather x1, blocking collectives, on_device(): lax.all_gather(last_row, ('req', 'head'), axis=1, tiled=True).reshape(-1, D)  81.9 us
    all_gather x1, waiting for transfers between devices, on_device(): lax.all_gather(mixed_rows, 'req', axis=0, tiled=True)  79.7 us
    psum x1, blocking collectives, on_device(): lax.psum(jnp.sum(jnp.exp(logits - row_max[:, None]), axis=1), ('req', 'he...  64.2 us
    pmax x1, blocking collectives, on_device(): row_max = lax.pmax(jnp.max(logits, axis=1), ('req', 'head'))  63.7 us
    psum x1, waiting for transfers between devices, on_device(): lax.psum(partial_rows.astype(jnp.bfloat16), 'head').astype(jnp.float32)  26.1 us
  transfers between devices with their start and end apart: 4, of which 4 were waited for; matrix products, arithmetic and copies ran while one was open for 0% of the time, Pallas kernels for 0%

commit v1 on v0

--- a/solution.py
+++ b/solution.py
@@ -144,7 +144,8 @@
     final_rows = norm_rows(collected, final_gain).astype(jnp.bfloat16)
     logits = jnp.dot(final_rows, w_vocab, preferred_element_type=jnp.float32)
     row_max = lax.pmax(jnp.max(logits, axis=1), ("req", "head"))
-    row_total = lax.psum(jnp.sum(jnp.exp(logits - row_max[:, None]), axis=1), ("req", "head"))
+    one_axis = lax.psum(jnp.sum(jnp.exp(logits - row_max[:, None]), axis=1), "head")
+    row_total = lax.psum(one_axis, "req")
     log_probs = logits - row_max[:, None] - jnp.log(row_total)[:, None]
     log_probs = jnp.take(log_probs, inverse_order(slot_request), axis=0)
     return (hidden_out, log_probs)

time: 748 us -> 861 us (1.15)
  the two profiles are of different devices: /device:TPU:1 before, /device:TPU:0 now
where the time goes in v1:
time: 861 us; the launch traced here: 860 us
  waiting for transfers between devices  508 us (59%)
  blocking collectives  277 us (32%)
  matrix products  33.1 us (4%)
  between operations  16.1 us (2%)
  local copies, waits for them, and re-layouts  13.3 us (2%)
  other arithmetic  12.9 us (1%)
    reduce_scatter x1, waiting for transfers between devices, on_device(): lax.psum_scatter(jnp.dot(active, w_down, preferred_element_type=jnp.float...  389 us
    psum x1, blocking collectives, on_device(): row_total = lax.psum(one_axis, 'req')  175 us
    all_gather x1, waiting for transfers between devices, on_device(): lax.all_gather(mixed_rows, 'req', axis=0, tiled=True)  80.2 us
    pmax x1, blocking collectives, on_device(): row_max = lax.pmax(jnp.max(logits, axis=1), ('req', 'head'))  64 us
    all_gather x1, blocking collectives, on_device(): lax.all_gather(last_row, ('req', 'head'), axis=1, tiled=True).reshape(-1, D)  32.5 us
    psum x1, waiting for transfers between devices, on_device(): lax.psum(partial_rows.astype(jnp.bfloat16), 'head').astype(jnp.float32)  25.6 us
  transfers between devices with their start and end apart: 4, of which 4 were waited for; matrix products, arithmetic and copies ran while one was open for 0% of the time, Pallas kernels for 0%

profile of v1, /device:TPU:0, one launch (start us, length us, event | category | flops | bytes accessed | tf_op | source)
XLA Modules:
  0.0 860.1 jit_solution(697221007026178037)
XLA Ops:
  7.2 0.0 copy-start
  7.2 0.0 reduce-scatter.3.cloned.1.call-start
  7.2 1.4 dynamic_slice.11
  10.6 1.2 dynamic_slice.12
  11.8 0.6 add_convert_fusion.2
  12.5 0.7 iota_compare_fusion.2
  13.2 1.1 multiply_reduce_fusion.1
  14.3 3.2 convolution_bitcast_fusion
  17.5 0.1 multiply_reduce_fusion.3
  17.7 0.0 copy-start.2
  17.7 0.1 copy.63
  17.8 0.1 copy.64
  17.9 0.2 multiply_cosine_fusion
  18.1 0.1 multiply_multiply_fusion
  18.2 0.2 subtract_convert_fusion
  18.5 0.0 copy-start.11
  18.5 4.0 reshape.165
  22.5 0.5 fusion.40
  23.0 0.1 multiply_reduce_fusion.4
  23.2 0.1 copy.68
  23.3 0.1 fusion.27
  23.4 0.1 subtract_convert_fusion.1
  23.5 4.1 reshape.167
  27.6 0.5 convolution_convert_fusion.2
  28.1 3.2 bitcast_reduce_fusion
  31.4 0.3 fusion.43
  31.8 1.4 fusion.12
  33.2 0.2 fusion.17
  33.4 0.1 copy.73
  33.6 0.1 convert_element_type.62
  33.7 3.8 convolution_convert_fusion.1
  37.5 0.0 reduce-scatter.3.cloned.1.call-update
  37.5 0.0 all-gather.2.cloned.1.call-start
  37.6 12.7 %reduce-scatter.3.cloned.1.call-done = bf16[64,1024]{1,0:T(8,128)(2,1)} async-done(((bf16[64,2048]{1,0:T(8,128)(2,1)}), bf16[64,1024]{1,0:T(8,128)(2,1)}) %reduce-scatter.3.cloned.1.call-update) | async-done | bytes 131088 | tf_op jit(solution)/shard_map/reduce_scatter | solution.py:116
  50.3 1.0 multiply_reduce_fusion.2
  51.3 2.6 psum.28
  53.9 1.7 multiply_convert_fusion.3
  55.6 0.0 all-gather.2.cloned.1.call-update
  55.6 0.0 all-reduce.2.cloned.1.call-start
  55.7 80.2 %all-gather.2.cloned.1.call-done = bf16[4096,1024]{1,0:T(8,128)(2,1)} async-done(((bf16[64,1024]{1,0:T(8,128)(2,1)}), bf16[4096,1024]{1,0:T(8,128)(2,1)}) %all-gather.2.cloned.1.call-update) | async-done | bytes 8388624 | tf_op jit(solution)/shard_map/all_gather | solution.py:125
  135.9 7.5 convolution_convert_fusion
  143.4 0.0 all-reduce.2.cloned.1.call-update
  143.4 0.0 reduce-scatter.5.cloned.1.call-start
  143.5 25.6 %all-reduce.2.cloned.1.call-done = bf16[4096,192]{0,1:T(8,128)(2,1)} async-done(((bf16[4096,192]{0,1:T(8,128)(2,1)}), bf16[4096,192]{0,1:T(8,128)(2,1)}) %all-reduce.2.cloned.1.call-update) | async-done | bytes 1572880 | tf_op jit(solution)/shard_map/psum | solution.py:129
  169.1 1.8 convert_element_type.67
  170.9 8.1 fusion.18
  179.0 0.0 reduce-scatter.5.cloned.1.call-update
  179.0 0.6 copy-done.14
  179.7 0.1 select_reduce_fusion
  179.8 389.0 %reduce-scatter.5.cloned.1.call-done = f32[64,1024]{1,0:T(8,128)} async-done(((f32[4096,1024]{1,0:T(8,128)}), f32[64,1024]{1,0:T(8,128)}) %reduce-scatter.5.cloned.1.call-update) | async-done | bytes 262160 | tf_op jit(solution)/shard_map/reduce_scatter | solution.py:134
  568.9 1.6 fusion.41
  570.5 32.5 %all_gather.7 = f32[1,131072]{1,0:T(1,128)S(1)} all-gather(f32[1,1024]{1,0:T(1,128)S(1)} %slice.36), channel_id=1, replica_groups=mesh['req'=64,'head'=2] {'req','head'}, dimensions={1}, use_global_device_ids=true | all-gather | bytes 528384 | tf_op jit(solution)/shard_map/all_gather | solution.py:143
  603.0 0.5 broadcast.162
  603.5 1.9 reduce.3
  605.4 0.1 reshape.169
  605.5 0.1 multiply_reduce_fusion
  605.6 4.2 fusion.44
  609.9 64.0 %pmax.7 = f32[64]{0:T(128)S(1)} all-reduce(f32[64]{0:T(128)S(1)} %get-tuple-element.14), channel_id=1, replica_groups=mesh['req'=64,'head'=2] {'req','head'}, use_global_device_ids=true, to_apply=%region_13.14 | all-reduce | flops 64 | bytes 512 | tf_op jit(solution)/shard_map/pmax | solution.py:146
  673.9 0.2 exponential_reduce_fusion
  674.2 2.5 psum.30
  676.6 175.3 %psum.31 = f32[64]{0:T(128)S(1)} all-reduce(f32[64]{0:T(128)S(1)} %psum.30), channel_id=1, replica_groups=mesh['req'=64,'head'=2] {'req'}, use_global_device_ids=true, to_apply=%region_16.17 | all-reduce | flops 64 | bytes 512 | tf_op jit(solution)/shard_map/psum | solution.py:148
  851.9 0.1 subtract_subtract_fusion
  852.0 0.7 gather_fusion
  852.7 0.8 broadcast_select_fusion
  (45 shorter events, 0.4 us)
Async XLA Ops:
  7.2 15.3 %copy-start = (bf16[2048,512]{1,0:T(8,128)(2,1)S(1)}, bf16[2048,512]{1,0:T(8,128)(2,1)}, u32[]{:S(2)}) copy-start(bf16[2048,512]{1,0:T(8,128)(2,1)} %param.21) | copy-start | bytes 6291460
  7.2 10.9 %copy-start.10 = (f32[128]{0:T(128)S(1)}, f32[128]{0:T(128)}, u32[]{:S(2)}) copy-start(f32[128]{0:T(128)} %param.23) | copy-start | bytes 1540
  7.2 43.1 %reduce-scatter.3.cloned.1.call-start = ((), (), s32[]{:S(2)}) async-start(), calls=%async_computation.2 | async-start | bytes 393216 | tf_op jit(solution)/shard_map/reduce_scatter | solution.py:116
  17.7 4.8 copy-start.2
  17.7 4.8 copy-start.7
  18.5 4.8 copy-start.11
  23.0 4.6 copy-start.3
  28.1 3.6 copy-start.4
  33.6 20.4 %copy-start.9 = (f32[1024]{0:T(1024)S(1)}, f32[1024]{0:T(1024)}, u32[]{:S(2)}) copy-start(f32[1024]{0:T(1024)} %param.30) | copy-start | bytes 12292
  33.6 102.3 %copy-start.12 = (bf16[1024,96]{0,1:T(8,128)(2,1)S(1)}, bf16[1024,96]{0,1:T(8,128)(2,1)}, u32[]{:S(2)}) copy-start(bf16[1024,96]{0,1:T(8,128)(2,1)} %param.32) | copy-start | bytes 589828
  33.7 102.2 %copy-start.13 = (bf16[1024,96]{0,1:T(8,128)(2,1)S(1)}, bf16[1024,96]{0,1:T(8,128)(2,1)}, u32[]{:S(2)}) copy-start(bf16[1024,96]{0,1:T(8,128)(2,1)} %param.31) | copy-start | bytes 589828
  37.5 98.4 %all-gather.2.cloned.1.call-start = ((), (), s32[]{:S(2)}) async-start(), calls=%async_computation.3 | async-start | bytes 8519680 | tf_op jit(solution)/shard_map/all_gather | solution.py:125
  55.6 113.5 %all-reduce.2.cloned.1.call-start = ((), (), s32[]{:S(2)}) async-start(), calls=%async_computation.4 | async-start | bytes 3145728 | tf_op jit(solution)/shard_map/psum | solution.py:129
  143.4 27.5 %copy-start.6 = (bf16[96,1024]{1,0:T(8,128)(2,1)S(1)}, bf16[96,1024]{1,0:T(8,128)(2,1)}, u32[]{:S(2)}) copy-start(bf16[96,1024]{1,0:T(8,128)(2,1)} %param.33) | copy-start | bytes 589828
  143.4 425.4 %reduce-scatter.5.cloned.1.call-start = ((), (), s32[]{:S(2)}) async-start(), calls=%async_computation.5 | async-start | bytes 17039360 | tf_op jit(solution)/shard_map/reduce_scatter | solution.py:134
  179.0 0.7 copy-start.14
  179.0 389.8 %copy-start.5 = (bf16[64,1024]{1,0:T(8,128)(2,1)S(1)}, bf16[64,1024]{1,0:T(8,128)(2,1)}, u32[]{:S(2)}) copy-start(bf16[64,1024]{1,0:T(8,128)(2,1)} %reduce-scatter.3.cloned.1.call-done) | copy-start | bytes 393220
  179.7 426.0 %copy-start.8 = (f32[2048]{0:T(1024)S(1)}, f32[2048]{0:T(1024)}, u32[]{:S(2)}) copy-start(f32[2048]{0:T(1024)} %param.34) | copy-start | bytes 24580
  605.6 247.9 %copy-start.1 = (bf16[2048,512]{1,0:T(8,128)(2,1)S(1)}, bf16[2048,512]{1,0:T(8,128)(2,1)}, u32[]{:S(2)}) copy-start(bf16[2048,512]{1,0:T(8,128)(2,1)} %param.21) | copy-start | bytes 6291460
Sparse Core Ops, SparseCore 0:
  37.6 12.6 reduce-scatter.2
  55.7 80.1 all-gather.1
  143.6 25.5 all-reduce.1
  179.2 389.6 reduce-scatter.4
